TPU v7x, 512 devices: a whole 4x8x8 slice. The times are simulated.
512 devices in a mesh: dp: 32 (over z, x), tensor: 16 (over y, core).
Axes of the slice: x: 4, y: 8, z: 8, core: 2. Of those that a mesh axis runs over, the one named last changes fastest.
Arguments:
- teacher_hidden: bfloat16 [512, 5120], P('dp', 'tensor'), may hold values from -200 to 200
- student_hidden: bfloat16 [512, 4096], P('dp', 'tensor'), may hold values from -8 to 8
- teacher_head: bfloat16 [5120, 131072], P(None, ('dp', 'tensor')), may hold values from -6 to 6
- student_head: bfloat16 [4096, 131072], P(None, ('dp', 'tensor')), may hold values from -6 to 6
- teacher_gain: float32 [5120], replicated, may hold values from 0.5 to 1.5
- lengths: int32 [64], replicated, may hold values from 1 to 8, as said below
- student_row: int32 [512], replicated, may hold values from 0 to 511, as said below
- targets: int32 [512], replicated, may hold values from 0 to 131071
Outputs:
- grad_logits: bfloat16 [512, 131072], P(None, ('dp', 'tensor'))
- divergence: float32 [512], P('dp')
- log_ratio: float32 [512], P('dp')
Inputs may be any that keep to these rules, and one draw needn't show every extreme that they name: The lengths of the 2 responses of one index of dp sum to at most 8, and to exactly 8 on some index. `student_row`: a permutation: every row of student_hidden is named once.
All inputs are finite; a program needn't handle non-finite values.
Results may differ from a plain program's by a relative error of at most 0.01095.
Values may be sent and summed in bfloat16 or wider, within the bound.
No kernel may reach another device: no remote copies, remote signals or barrier semaphores. Data moves between devices by JAX's collectives and lax.ppermute only.
A program may use at most 64 MiB of HBM per device.

v0:
```python
import functools

import jax
import jax.numpy as jnp
from jax import lax
from jax.experimental import pallas as pl
from jax.experimental.pallas import tpu as pltpu
from jax.sharding import Mesh
from jax.sharding import PartitionSpec as P


SLOT = 8
LIVE_DEV = 8
DP = ("dp_0", "dp_1")
TENSOR = ("tensor_0", "tensor_1")
DP_TENSOR = ("dp_0", "dp_1", "tensor_0", "tensor_1")


def spread(array, axes):
    count = lax.axis_size(axes)
    return lax.all_to_all(jnp.broadcast_to(array, (count, *array.shape)), axes, 0, 0)


def shifted(array, axis, by):
    count = lax.axis_size(axis)
    return lax.ppermute(array, axis, [(i, (i + by) % count) for i in range(count)])


def ring_pieces(piece, axis):
    count = lax.axis_size(axis)
    found = [(0, piece)]
    ahead = behind = piece
    for k in range(1, count // 2):
        ahead, behind = shifted(ahead, axis, 1), shifted(behind, axis, -1)
        found += [(-k, ahead), (k, behind)]
    return found + [(-(count // 2), shifted(ahead, axis, 1))]


VMEM = pl.BlockSpec(memory_space=pltpu.VMEM)
SMEM = pl.BlockSpec(memory_space=pltpu.SMEM)
ANY = pl.BlockSpec(memory_space=pl.ANY)
TERMS = 3


def pack_kernel(lengths, teacher, student, packed):
    group = lax.axis_index("dp_0") * lax.axis_size("dp_1") + lax.axis_index("dp_1")
    first, second = lengths[2 * group], lengths[2 * group + 1]
    half, s_width = student.shape[0] // 2, student.shape[1]
    grid = (LIVE_DEV, teacher.shape[0])
    slot, row = (lax.broadcasted_iota(jnp.int32, grid, d) for d in range(2))
    place = jnp.where(slot < first, slot, SLOT + slot - first)
    pick = jnp.where((place == row) & (slot < first + second), 1.0, 0.0)
    chosen = jnp.dot(
        pick.astype(jnp.bfloat16), teacher[...], preferred_element_type=jnp.float32
    ).astype(jnp.bfloat16)
    low, high = student[:half, :], student[half:, :]
    for i in range(packed.shape[0]):
        packed[i, :, :s_width] = low
        packed[i, :, s_width : 2 * s_width] = high
        packed[i, :, 2 * s_width :] = chosen


def choose_kernel(half, s_width, source, gains, everyone, piece):
    count = everyone.shape[0]
    t_width = everyone.shape[1] - 2 * s_width
    wide = lax.axis_index("tensor_0") * lax.axis_size("tensor_1") + lax.axis_index("tensor_1")
    j = lax.broadcasted_iota(jnp.int32, (count, count), 1)
    low = (j // half) * (2 * half) + j % half
    want = jnp.broadcast_to(source[:, :1], (count, count))
    one = lambda hit: jnp.where(hit, 1.0, 0.0).astype(jnp.bfloat16)
    dot = functools.partial(jnp.dot, preferred_element_type=jnp.float32)
    chosen = dot(one(want == low), everyone[:, :s_width])
    chosen += dot(one(want == low + half), everyone[:, s_width : 2 * s_width])
    piece[:, :s_width] = chosen.astype(jnp.bfloat16)
    values = everyone[:, 2 * s_width :].astype(jnp.float32)
    piece[:, s_width : s_width + t_width] = (values * gains[pl.ds(wide, 1), :]).astype(jnp.bfloat16)
    rest = jnp.sum(values * values, axis=1, keepdims=True)
    at = s_width + t_width
    for k in range(TERMS):
        term = rest.astype(jnp.bfloat16)
        piece[:, at + k : at + k + 1] = term
        rest = rest - term.astype(jnp.float32)


def block_kernel(offsets, had, t_width, s_width, *refs):
    n = len(offsets)
    blocks, refs = refs[:n], refs[n:]
    t_head, s_head, t_twin, s_twin = refs[:4]
    refs = refs[4:]
    if had:
        before, refs = refs[:2], refs[2:]
    mine, sent, t_own_buf, s_own_buf, t_twin_buf, s_twin_buf, sems = refs
    y, core = lax.axis_index("tensor_0"), lax.axis_index("tensor_1")
    ys, cores = lax.axis_size("tensor_0"), lax.axis_size("tensor_1")
    vocab = t_head.shape[1]
    copies = []
    for i, offset in enumerate(offsets):
        at = lax.rem(y + (offset % ys), ys)
        wide = at * cores + core
        froms = (
            t_head.at[pl.ds(pl.multiple_of(wide * t_width, 64), t_width), :],
            s_head.at[pl.ds(pl.multiple_of(wide * s_width, 64), s_width), :],
            t_twin.at[at],
            s_twin.at[at],
        )
        tos = (t_own_buf.at[i], s_own_buf.at[i], t_twin_buf.at[i], s_twin_buf.at[i])
        for k in range(4):
            copy = pltpu.make_async_copy(froms[k], tos[k], sems.at[i, k])
            copy.start()
            copies.append(copy)
    t_mine = s_mine = t_sent = s_sent = squares = None
    dot = functools.partial(jnp.dot, preferred_element_type=jnp.float32)
    if had:
        t_mine, s_mine = before[0][:, :vocab], before[0][:, vocab:]
        t_sent, s_sent = before[1][:, :vocab], before[1][:, vocab : 2 * vocab]
        squares = before[1][:, 2 * vocab : 2 * vocab + 1]
    plus = lambda total, term: term if total is None else total + term
    for i in range(n):
        for k in range(4):
            copies[4 * i + k].wait()
        at = s_width + t_width
        for k in range(TERMS):
            squares = plus(squares, blocks[i][:, at + k : at + k + 1].astype(jnp.float32))
        student, scaled = blocks[i][:, :s_width], blocks[i][:, s_width:at]
        t_mine = plus(t_mine, dot(scaled, t_own_buf[i]))
        t_sent = plus(t_sent, dot(scaled, t_twin_buf[i]))
        s_mine = plus(s_mine, dot(student, s_own_buf[i]))
        s_sent = plus(s_sent, dot(student, s_twin_buf[i]))
    mine[:, :vocab], mine[:, vocab:] = t_mine, s_mine
    sent[:, :vocab], sent[:, vocab : 2 * vocab] = t_sent, s_sent
    sent[:, 2 * vocab :] = jnp.broadcast_to(squares, (squares.shape[0], 128))


def block_products(found, heads, before):
    offsets, blocks = [f[0] for f in found], [f[1] for f in found]
    n, rows, vocab = len(found), blocks[0].shape[0], heads[0].shape[1]
    t_width, s_width = heads[2].shape[1], heads[3].shape[1]
    had = before is not None
    bf16 = jnp.bfloat16
    return pl.pallas_call(
        functools.partial(block_kernel, offsets, had, t_width, s_width),
        out_shape=(
            jax.ShapeDtypeStruct((rows, 2 * vocab), jnp.float32),
            jax.ShapeDtypeStruct((rows, 2 * vocab + 128), jnp.float32),
        ),
        in_specs=[VMEM] * n + [ANY] * 4 + [VMEM] * (2 if had else 0),
        out_specs=(VMEM, VMEM),
        scratch_shapes=[
            pltpu.VMEM((n, t_width, vocab), bf16),
            pltpu.VMEM((n, s_width, vocab), bf16),
            pltpu.VMEM((n, t_width, vocab), bf16),
            pltpu.VMEM((n, s_width, vocab), bf16),
            pltpu.SemaphoreType.DMA((n, 4)),
        ],
        compiler_params=pltpu.CompilerParams(vmem_limit_bytes=24 << 20),
        cost_estimate=pl.CostEstimate(
            flops=4 * n * rows * vocab * (t_width + s_width),
            bytes_accessed=4 * n * vocab * (t_width + s_width),
            transcendentals=0,
        ),
    )(*blocks, *heads, *(before if had else ()))


def merge(parts):
    teacher, student, mean, picked = (parts[:, k] for k in range(4))
    top_t, top_s = jnp.max(teacher, axis=0), jnp.max(student, axis=0)
    sum_t = jnp.sum(jnp.exp(teacher - top_t), axis=0)
    weight = jnp.exp(student - top_s)
    sum_s = jnp.sum(weight, axis=0)
    mean = jnp.sum(weight * mean, axis=0) / sum_s
    return jnp.stack([top_t + jnp.log(sum_t), top_s + jnp.log(sum_s), mean, jnp.sum(picked, axis=0)])


def on_device(
    teacher_hidden,
    student_hidden,
    teacher_head,
    student_head,
    teacher_gain,
    lengths,
    student_row,
    targets,
):
    dp_count = lax.axis_size(DP)
    tensor_count = lax.axis_size(TENSOR)
    y_count, core_count = (lax.axis_size(a) for a in TENSOR)
    local_tokens, t_width = teacher_hidden.shape
    s_width = student_hidden.shape[1]
    token_count = local_tokens * dp_count
    vocab_local = teacher_head.shape[1]
    dp_index = lax.axis_index(DP)
    core = lax.axis_index("tensor_1")
    vocab_start = (dp_index * tensor_count + lax.axis_index(TENSOR)) * vocab_local

    first, second = lengths.reshape(dp_count, 2)[:, :1], lengths.reshape(dp_count, 2)[:, 1:]
    slot = jnp.arange(LIVE_DEV, dtype=jnp.int32)[None, :]
    place = jnp.where(slot < first, slot, SLOT + slot - first)
    live = slot < first + second
    group = jnp.arange(dp_count, dtype=jnp.int32)[:, None] * local_tokens
    row_token = jnp.where(live, group + place, -1).reshape(-1)
    row_live = live.reshape(-1).astype(jnp.float32)
    rows = row_token.shape[0]

    half = local_tokens // 2
    packed = pl.pallas_call(
        pack_kernel,
        out_shape=jax.ShapeDtypeStruct((dp_count, half, 2 * s_width + t_width), jnp.bfloat16),
        in_specs=[SMEM, VMEM, VMEM],
        out_specs=VMEM,
        compiler_params=pltpu.CompilerParams(vmem_limit_bytes=8 << 20),
    )(lengths, teacher_hidden, student_hidden)
    t_blocks = teacher_head.reshape(y_count, core_count, t_width, vocab_local)
    s_blocks = student_head.reshape(y_count, core_count, s_width, vocab_local)
    other = lambda blocks: lax.dynamic_index_in_dim(blocks, 1 - core, 1, keepdims=False)
    twins = [shifted(other(blocks), "tensor_1", 1) for blocks in (t_blocks, s_blocks)]
    heads = (teacher_head, student_head, *twins)
    gains = teacher_gain.reshape(tensor_count, t_width)
    everyone = lax.all_to_all(packed, DP, 0, 0)

    token_of = row_token[:, None] == jnp.arange(token_count, dtype=jnp.int32)[None, :]
    row_source = jnp.sum(jnp.where(token_of, student_row[None, :], 0), axis=1)
    row_target = jnp.sum(jnp.where(token_of, targets[None, :], 0), axis=1)
    piece = pl.pallas_call(
        functools.partial(choose_kernel, half, s_width),
        out_shape=jax.ShapeDtypeStruct((rows, s_width + t_width + TERMS), jnp.bfloat16),
        in_specs=[VMEM] * 3,
        out_specs=VMEM,
        compiler_params=pltpu.CompilerParams(vmem_limit_bytes=8 << 20),
    )(jnp.broadcast_to(row_source[:, None], (rows, 128)), gains, everyone.reshape(rows, -1))

    found = ring_pieces(piece, "tensor_0")
    early = 1 + 2 * 2
    mine, sent = block_products(found[:early], heads, None)
    mine, sent = block_products(found[early:], heads, (mine, sent))
    squares = sent[:, 2 * vocab_local :][:, :1]
    got = shifted(sent, "tensor_1", 1)
    mean_square = (squares + got[:, 2 * vocab_local :][:, :1]) / (t_width * tensor_count)
    row_scale = lax.rsqrt(mean_square + 1e-06)
    both = mine + got[:, : 2 * vocab_local]
    teacher_logits = both[:, :vocab_local] * row_scale
    student_logits = both[:, vocab_local:]

    gap = student_logits - teacher_logits
    hits = (row_target - vocab_start)[:, None] == jnp.arange(vocab_local, dtype=jnp.int32)[None, :]
    picked = jnp.sum(jnp.where(hits, gap, 0.0), axis=1)
    teacher_max = jnp.max(teacher_logits, axis=1)
    student_max = jnp.max(student_logits, axis=1)
    teacher_sum = jnp.sum(jnp.exp(teacher_logits - teacher_max[:, None]), axis=1)
    student_exp = jnp.exp(student_logits - student_max[:, None])
    student_sum = jnp.sum(student_exp, axis=1)
    mean = jnp.sum(student_exp * gap, axis=1) / student_sum
    local = jnp.stack(
        [teacher_max + jnp.log(teacher_sum), student_max + jnp.log(student_sum), mean, picked]
    )
    merged = merge(spread(merge(spread(local, DP)), TENSOR))
    teacher_lse, student_lse, mean, picked = (merged[k] for k in range(4))

    student_prob = jnp.exp(student_logits - student_lse[:, None])
    gradient = (row_live[:, None] * student_prob * (gap - mean[:, None])).astype(jnp.bfloat16)
    lse_gap = teacher_lse - student_lse
    token_ids = jnp.arange(token_count, dtype=jnp.int32)
    unpack = (token_ids[:, None] == row_token[None, :]).astype(jnp.bfloat16)
    grad_logits = jnp.dot(unpack, gradient, preferred_element_type=jnp.float32).astype(jnp.bfloat16)
    own_ids = dp_index * local_tokens + jnp.arange(local_tokens, dtype=jnp.int32)
    own_of = own_ids[:, None] == row_token[None, :]
    divergence = jnp.sum(jnp.where(own_of, (mean + lse_gap)[None, :], 0.0), axis=1)
    log_ratio = jnp.sum(jnp.where(own_of, (picked + lse_gap)[None, :], 0.0), axis=1)
    return (grad_logits, divergence, log_ratio)


def solution(mesh):
    finer = Mesh(mesh.devices.reshape(8, 4, 8, 2), ("dp_0", "dp_1", "tensor_0", "tensor_1"))
    in_specs = (
        P(DP, TENSOR),
        P(DP, TENSOR),
        P(None, DP_TENSOR),
        P(None, DP_TENSOR),
        P(),
        P(),
        P(),
        P(),
    )
    out_specs = (P(None, DP_TENSOR), P(DP), P(DP))
    return jax.shard_map(
        on_device, mesh=finer, in_specs=in_specs, out_specs=out_specs, check_vma=False
    )
```

profile of v0, /device:TPU:1, one launch (start us, length us, event | category | flops | bytes accessed | tf_op | source)
XLA Modules:
  0.0 128.7 jit_solution(10708318598714268382)
XLA Ops:
  0.7 2.5 %dynamic-slice_bitcast_fusion = bf16[8,320,256]{2,1,0:T(8,128)(2,1)} fusion(bf16[8,2,320,256]{3,2,1,0:T(8,128)(2,1)} %bitcast.59, s32[]{:T(128)S(6)} %select_n.51), kind=kLoop, calls=%fused_computation | loop fusion | bytes 2621444 | tf_op jit(solution)/shard_map/jit(dynamic_index_in_dim)/squeeze | solution.py:214
  3.2 8.7 %collective-permute-start.7 = (bf16[8,320,256]{2,1,0:T(8,128)(2,1)}, bf16[8,320,256]{2,1,0:T(8,128)(2,1)}, u32[]{:S(2)}, u32[]{:S(2)}) collective-permute-start(bf16[8,320,256]{2,1,0:T(8,128)(2,1)} %dynamic-slice_bitcast_fusion), channel_id=1, source_target_pairs={{0,1},{1,0},{2,3},{3,2},{4,5},{5,4},{6,7},{7,6},{8,9},{9,8},{10,11... | collective-permute-start | bytes 3932168 | tf_op jit(solution)/shard_map/ppermute | solution.py:26
  12.0 1.5 %shard_map.103 = bf16[32,8,832]{2,1,0:T(8,128)(2,1)} custom-call(s32[64]{0:T(128)S(1)} %copy-done.4, bf16[16,320]{1,0:T(8,128)(2,1)S(1)} %copy-done.2, bf16[16,256]{1,0:T(8,128)(2,1)S(1)} %copy-done.3), custom_call_target="tpu_custom_call" | custom-call | tf_op jit(solution)/shard_map/pallas_call | solution.py:205
  13.5 7.8 %all-to-all-start = ((bf16[32,8,832]{2,1,0:T(8,128)(2,1)}), bf16[32,8,832]{2,1,0:T(8,128)(2,1)S(1)}, u32[]{:S(2)}, u32[]{:S(2)}) async-start(bf16[32,8,832]{2,1,0:T(8,128)(2,1)} %shard_map.103), calls=%async_computation | async-start | bytes 917504 | tf_op jit(solution)/shard_map/all_to_all | solution.py:218
  21.3 0.1 reshape.293
  21.4 0.2 slice_reduce_fusion.3
  21.6 0.1 lt.71
  21.6 0.1 lt.72
  21.7 0.1 lt.69
  21.8 0.1 lt.75
  21.9 0.1 lt.76
  22.0 0.1 add.158
  22.1 0.1 add.159
  22.2 0.1 sub.113
  22.3 0.1 reshape.294.gains
  22.4 0.3 select_reduce_fusion
  22.7 14.2 %all-to-all-done = bf16[32,8,832]{2,1,0:T(8,128)(2,1)S(1)} async-done(((bf16[32,8,832]{2,1,0:T(8,128)(2,1)}), bf16[32,8,832]{2,1,0:T(8,128)(2,1)S(1)}, u32[]{:S(2)}, u32[]{:S(2)}) %all-to-all-start) | async-done | bytes 426016 | tf_op jit(solution)/shard_map/all_to_all | solution.py:218
  36.9 0.1 broadcast_in_dim.83.source
  36.9 0.3 shard_map.104.refs_0_
  37.2 3.2 %collective-permute-start = (bf16[256,579]{1,0:T(8,128)(2,1)S(1)}, bf16[256,579]{1,0:T(8,128)(2,1)S(1)}, u32[]{:S(2)}, u32[]{:S(2)}) collective-permute-start(bf16[256,579]{1,0:T(8,128)(2,1)S(1)} %shard_map.104.refs_0_), channel_id=1, source_target_pairs={{0,2},{2,4},{4,6},{6,8},{8,10},{10,12},{12,14},{14,0},{1,3},{3,5},... | collective-permute-start | bytes 889352 | tf_op jit(solution)/shard_map/ppermute | solution.py:26
  40.5 1.3 %dynamic-slice_bitcast_fusion.1 = bf16[8,256,256]{2,1,0:T(8,128)(2,1)S(1)} fusion(bf16[8,2,256,256]{3,2,1,0:T(8,128)(2,1)} %bitcast.60, s32[]{:T(128)S(6)} %select_n.51), kind=kLoop, calls=%fused_computation.2 | loop fusion | bytes 2097156 | tf_op jit(solution)/shard_map/jit(dynamic_index_in_dim)/squeeze | solution.py:214
  41.8 4.0 %collective-permute-start.8 = (bf16[8,256,256]{2,1,0:T(8,128)(2,1)S(1)}, bf16[8,256,256]{2,1,0:T(8,128)(2,1)S(1)}, u32[]{:S(2)}, u32[]{:S(2)}) collective-permute-start(bf16[8,256,256]{2,1,0:T(8,128)(2,1)S(1)} %dynamic-slice_bitcast_fusion.1), channel_id=1, source_target_pairs={{0,1},{1,0},{2,3},{3,2},{4,5},{5,4},{6,7},{7,6},{8,9},{9,8},{10,11... | collective-permute-start | bytes 3145736 | tf_op jit(solution)/shard_map/ppermute | solution.py:26
  45.8 3.5 %collective-permute-start.3 = (bf16[256,579]{1,0:T(8,128)(2,1)S(1)}, bf16[256,579]{1,0:T(8,128)(2,1)S(1)}, u32[]{:S(2)}, u32[]{:S(2)}) collective-permute-start(bf16[256,579]{1,0:T(8,128)(2,1)S(1)} %shard_map.104.refs_0_), channel_id=1, source_target_pairs={{0,14},{2,0},{4,2},{6,4},{8,6},{10,8},{12,10},{14,12},{1,15},{3,1}... | collective-permute-start | bytes 889352 | tf_op jit(solution)/shard_map/ppermute | solution.py:26
  49.4 1.9 %collective-permute-start.1 = (bf16[256,579]{1,0:T(8,128)(2,1)S(1)}, bf16[256,579]{1,0:T(8,128)(2,1)S(1)}, u32[]{:S(2)}, u32[]{:S(2)}) collective-permute-start(bf16[256,579]{1,0:T(8,128)(2,1)S(1)} %collective-permute-done.refs_1_), channel_id=1, source_target_pairs={{0,2},{2,4},{4,6},{6,8},{8,10},{10,12},{12,14},{14,0},{1,3},{3,5},... | collective-permute-start | bytes 889352 | tf_op jit(solution)/shard_map/ppermute | solution.py:26
  51.3 5.7 %collective-permute-done.3.refs_2_ = bf16[256,579]{1,0:T(8,128)(2,1)S(1)} collective-permute-done((bf16[256,579]{1,0:T(8,128)(2,1)S(1)}, bf16[256,579]{1,0:T(8,128)(2,1)S(1)}, u32[]{:S(2)}, u32[]{:S(2)}) %collective-permute-start.3) | collective-permute-done | bytes 296480 | tf_op jit(solution)/shard_map/ppermute | solution.py:26
  57.0 4.7 %collective-permute-start.4 = (bf16[256,579]{1,0:T(8,128)(2,1)S(1)}, bf16[256,579]{1,0:T(8,128)(2,1)S(1)}, u32[]{:S(2)}, u32[]{:S(2)}) collective-permute-start(bf16[256,579]{1,0:T(8,128)(2,1)S(1)} %collective-permute-done.3.refs_2_), channel_id=1, source_target_pairs={{0,14},{2,0},{4,2},{6,4},{8,6},{10,8},{12,10},{14,12},{1,15},{3,1}... | collective-permute-start | bytes 889352 | tf_op jit(solution)/shard_map/ppermute | solution.py:26
  61.7 1.9 %collective-permute-start.2 = (bf16[256,579]{1,0:T(8,128)(2,1)S(1)}, bf16[256,579]{1,0:T(8,128)(2,1)S(1)}, u32[]{:S(2)}, u32[]{:S(2)}) collective-permute-start(bf16[256,579]{1,0:T(8,128)(2,1)S(1)} %collective-permute-done.1.refs_3_), channel_id=1, source_target_pairs={{0,2},{2,4},{4,6},{6,8},{8,10},{10,12},{12,14},{14,0},{1,3},{3,5},... | collective-permute-start | bytes 889352 | tf_op jit(solution)/shard_map/ppermute | solution.py:26
  63.6 4.2 %collective-permute-done.4.refs_4_ = bf16[256,579]{1,0:T(8,128)(2,1)S(1)} collective-permute-done((bf16[256,579]{1,0:T(8,128)(2,1)S(1)}, bf16[256,579]{1,0:T(8,128)(2,1)S(1)}, u32[]{:S(2)}, u32[]{:S(2)}) %collective-permute-start.4) | collective-permute-done | bytes 296480 | tf_op jit(solution)/shard_map/ppermute | solution.py:26
  67.9 5.3 %collective-permute-start.5 = (bf16[256,579]{1,0:T(8,128)(2,1)S(1)}, bf16[256,579]{1,0:T(8,128)(2,1)S(1)}, u32[]{:S(2)}, u32[]{:S(2)}) collective-permute-start(bf16[256,579]{1,0:T(8,128)(2,1)S(1)} %collective-permute-done.4.refs_4_), channel_id=1, source_target_pairs={{0,14},{2,0},{4,2},{6,4},{8,6},{10,8},{12,10},{14,12},{1,15},{3,1}... | collective-permute-start | bytes 889352 | tf_op jit(solution)/shard_map/ppermute | solution.py:26
  73.2 1.9 %collective-permute-start.6 = (bf16[256,579]{1,0:T(8,128)(2,1)S(1)}, bf16[256,579]{1,0:T(8,128)(2,1)S(1)}, u32[]{:S(2)}, u32[]{:S(2)}) collective-permute-start(bf16[256,579]{1,0:T(8,128)(2,1)S(1)} %collective-permute-done.2.refs_0_), channel_id=1, source_target_pairs={{0,2},{2,4},{4,6},{6,8},{8,10},{10,12},{12,14},{14,0},{1,3},{3,5},... | collective-permute-start | bytes 889352 | tf_op jit(solution)/shard_map/ppermute | solution.py:26
  75.2 1.6 %copy-done.1 = bf16[4096,256]{1,0:T(8,128)(2,1)S(1)} copy-done((bf16[4096,256]{1,0:T(8,128)(2,1)S(1)}, bf16[4096,256]{1,0:T(8,128)(2,1)}, u32[]{:S(2)}) %copy-start.1) | copy-done | bytes 2097176
  76.8 4.4 %shard_map.105 = (f32[256,512]{1,0:T(8,128)S(1)}, f32[256,640]{1,0:T(8,128)S(1)}) custom-call(bf16[256,579]{1,0:T(8,128)(2,1)S(1)} %shard_map.104.refs_0_, bf16[256,579]{1,0:T(8,128)(2,1)S(1)} %collective-permute-done.refs_1_, bf16[256,579]{1,0:T(8,128)(2,1)S(1)} %collective-permute-done.3.refs_2_, bf16[256,579]{1,0:T(8,128)(2,1)S(1)} %collective-permute-done.1.refs_3_, ...), custom_call_target="tpu_custom_call" | custom-call | flops 754974720 | bytes 2949120 | tf_op jit(solution)/shard_map/pallas_call | solution.py:140
  81.2 2.4 %collective-permute-done.6.refs_2_ = bf16[256,579]{1,0:T(8,128)(2,1)S(1)} collective-permute-done((bf16[256,579]{1,0:T(8,128)(2,1)S(1)}, bf16[256,579]{1,0:T(8,128)(2,1)S(1)}, u32[]{:S(2)}, u32[]{:S(2)}) %collective-permute-start.6) | collective-permute-done | bytes 296480 | tf_op jit(solution)/shard_map/ppermute | solution.py:26
  83.6 3.7 %shard_map.106 = (f32[256,512]{1,0:T(8,128)S(1)}, f32[256,640]{1,0:T(8,128)}) custom-call(bf16[256,579]{1,0:T(8,128)(2,1)S(1)} %collective-permute-done.2.refs_0_, bf16[256,579]{1,0:T(8,128)(2,1)S(1)} %collective-permute-done.5.refs_1_, bf16[256,579]{1,0:T(8,128)(2,1)S(1)} %collective-permute-done.6.refs_2_, bf16[5120,256]{1,0:T(8,128)(2,1)S(1)} %copy-done, ...), custom_call_target="tpu_custom_call" | custom-call | flops 452984832 | bytes 1769472 | tf_op jit(solution)/shard_map/pallas_call | solution.py:140
  87.3 4.8 %collective-permute-start.9 = (f32[256,640]{1,0:T(8,128)}, f32[256,640]{1,0:T(8,128)S(1)}, u32[]{:S(2)}, u32[]{:S(2)}) collective-permute-start(f32[256,640]{1,0:T(8,128)} %get-tuple-element.10), channel_id=1, source_target_pairs={{0,1},{1,0},{2,3},{3,2},{4,5},{5,4},{6,7},{7,6},{8,9},{9,8},{10,11... | collective-permute-start | bytes 1966088 | tf_op jit(solution)/shard_map/ppermute | solution.py:26
  92.1 1.9 %collective-permute-done.9 = f32[256,640]{1,0:T(8,128)S(1)} collective-permute-done((f32[256,640]{1,0:T(8,128)}, f32[256,640]{1,0:T(8,128)S(1)}, u32[]{:S(2)}, u32[]{:S(2)}) %collective-permute-start.9) | collective-permute-done | bytes 655392 | tf_op jit(solution)/shard_map/ppermute | solution.py:26
  94.0 1.0 fusion.7
  95.0 0.1 slice_add_fusion
  95.1 0.2 fusion.3
  95.3 0.4 fusion.1
  95.8 13.4 %all_to_all.15 = f32[32,4,256]{2,1,0:T(4,128)S(1)} all-to-all(f32[32,4,256]{2,1,0:T(4,128)S(1)} %broadcast_in_dim.86), channel_id=1, replica_groups=mesh['dp_0'=8,'dp_1'=4,'tensor_0'=8,'tensor_1'=2] {'dp_0','dp_1'}, dimensions={0} | all-to-all | bytes 262144 | tf_op jit(solution)/shard_map/all_to_all | solution.py:21
  109.2 0.1 slice_reduce_fusion.7
  109.4 0.6 broadcast_in_dim.87
  110.1 9.0 %all-to-all-start.2 = ((f32[16,4,256]{2,1,0:T(4,128)}), f32[16,4,256]{2,1,0:T(4,128)S(1)}, u32[]{:S(2)}, u32[]{:S(2)}) async-start(f32[16,4,256]{2,1,0:T(4,128)} %broadcast_in_dim.87), calls=%async_computation.2 | async-start | bytes 131072 | tf_op jit(solution)/shard_map/all_to_all | solution.py:21
  119.0 7.8 %all-to-all-done.2 = f32[16,4,256]{2,1,0:T(4,128)S(1)} async-done(((f32[16,4,256]{2,1,0:T(4,128)}), f32[16,4,256]{2,1,0:T(4,128)S(1)}, u32[]{:S(2)}, u32[]{:S(2)}) %all-to-all-start.2) | async-done | bytes 65568 | tf_op jit(solution)/shard_map/all_to_all | solution.py:21
  126.8 0.1 slice_reduce_fusion.2
  127.0 0.7 fusion.18
  127.7 1.1 convolution_convert_fusion
  (41 shorter events, 0.3 us)
Async XLA Ops:
  0.6 11.3 %copy-start.4 = (s32[64]{0:T(128)S(1)}, s32[64]{0:T(128)}, u32[]{:S(2)}) copy-start(s32[64]{0:T(128)} %lengths.1) | copy-start | bytes 772
  0.6 11.3 %copy-start.2 = (bf16[16,320]{1,0:T(8,128)(2,1)S(1)}, bf16[16,320]{1,0:T(8,128)(2,1)}, u32[]{:S(2)}) copy-start(bf16[16,320]{1,0:T(8,128)(2,1)} %teacher.1) | copy-start | bytes 30724
  0.7 11.3 %copy-start.3 = (bf16[16,256]{1,0:T(8,128)(2,1)S(1)}, bf16[16,256]{1,0:T(8,128)(2,1)}, u32[]{:S(2)}) copy-start(bf16[16,256]{1,0:T(8,128)(2,1)} %student.1) | copy-start | bytes 24580
  0.7 21.6 %copy-start.5 = (f32[5120]{0:T(1024)S(1)}, f32[5120]{0:T(1024)}, u32[]{:S(2)}) copy-start(f32[5120]{0:T(1024)} %param.12) | copy-start | bytes 61444
  0.7 21.7 %copy-start.6 = (s32[512]{0:T(512)S(1)}, s32[512]{0:T(512)}, u32[]{:S(2)}) copy-start(s32[512]{0:T(512)} %param.15) | copy-start | bytes 6148
  0.7 21.7 %copy-start.7 = (s32[512]{0:T(512)S(1)}, s32[512]{0:T(512)}, u32[]{:S(2)}) copy-start(s32[512]{0:T(512)} %param.14) | copy-start | bytes 6148
  3.2 71.9 %collective-permute-start.7 = (bf16[8,320,256]{2,1,0:T(8,128)(2,1)}, bf16[8,320,256]{2,1,0:T(8,128)(2,1)}, u32[]{:S(2)}, u32[]{:S(2)}) collective-permute-start(bf16[8,320,256]{2,1,0:T(8,128)(2,1)} %dynamic-slice_bitcast_fusion), channel_id=1, source_target_pairs={{0,1},{1,0},{2,3},{3,2},{4,5},{5,4},{6,7},{7,6},{8,9},{9,8},{10,11... | collective-permute-start | bytes 3932168 | tf_op jit(solution)/shard_map/ppermute | solution.py:26
  13.5 61.7 %copy-start = (bf16[5120,256]{1,0:T(8,128)(2,1)S(1)}, bf16[5120,256]{1,0:T(8,128)(2,1)}, u32[]{:S(2)}) copy-start(bf16[5120,256]{1,0:T(8,128)(2,1)} %refs_3_.1) | copy-start | bytes 7864324
  13.5 23.4 %all-to-all-start = ((bf16[32,8,832]{2,1,0:T(8,128)(2,1)}), bf16[32,8,832]{2,1,0:T(8,128)(2,1)S(1)}, u32[]{:S(2)}, u32[]{:S(2)}) async-start(bf16[32,8,832]{2,1,0:T(8,128)(2,1)} %shard_map.103), calls=%async_computation | async-start | bytes 917504 | tf_op jit(solution)/shard_map/all_to_all | solution.py:218
  37.2 12.1 %collective-permute-start = (bf16[256,579]{1,0:T(8,128)(2,1)S(1)}, bf16[256,579]{1,0:T(8,128)(2,1)S(1)}, u32[]{:S(2)}, u32[]{:S(2)}) collective-permute-start(bf16[256,579]{1,0:T(8,128)(2,1)S(1)} %shard_map.104.refs_0_), channel_id=1, source_target_pairs={{0,2},{2,4},{4,6},{6,8},{8,10},{10,12},{12,14},{14,0},{1,3},{3,5},... | collective-permute-start | bytes 889352 | tf_op jit(solution)/shard_map/ppermute | solution.py:26
  41.8 33.4 %collective-permute-start.8 = (bf16[8,256,256]{2,1,0:T(8,128)(2,1)S(1)}, bf16[8,256,256]{2,1,0:T(8,128)(2,1)S(1)}, u32[]{:S(2)}, u32[]{:S(2)}) collective-permute-start(bf16[8,256,256]{2,1,0:T(8,128)(2,1)S(1)} %dynamic-slice_bitcast_fusion.1), channel_id=1, source_target_pairs={{0,1},{1,0},{2,3},{3,2},{4,5},{5,4},{6,7},{7,6},{8,9},{9,8},{10,11... | collective-permute-start | bytes 3145736 | tf_op jit(solution)/shard_map/ppermute | solution.py:26
  45.8 11.1 %collective-permute-start.3 = (bf16[256,579]{1,0:T(8,128)(2,1)S(1)}, bf16[256,579]{1,0:T(8,128)(2,1)S(1)}, u32[]{:S(2)}, u32[]{:S(2)}) collective-permute-start(bf16[256,579]{1,0:T(8,128)(2,1)S(1)} %shard_map.104.refs_0_), channel_id=1, source_target_pairs={{0,14},{2,0},{4,2},{6,4},{8,6},{10,8},{12,10},{14,12},{1,15},{3,1}... | collective-permute-start | bytes 889352 | tf_op jit(solution)/shard_map/ppermute | solution.py:26
  49.4 12.3 %collective-permute-start.1 = (bf16[256,579]{1,0:T(8,128)(2,1)S(1)}, bf16[256,579]{1,0:T(8,128)(2,1)S(1)}, u32[]{:S(2)}, u32[]{:S(2)}) collective-permute-start(bf16[256,579]{1,0:T(8,128)(2,1)S(1)} %collective-permute-done.refs_1_), channel_id=1, source_target_pairs={{0,2},{2,4},{4,6},{6,8},{8,10},{10,12},{12,14},{14,0},{1,3},{3,5},... | collective-permute-start | bytes 889352 | tf_op jit(solution)/shard_map/ppermute | solution.py:26
  57.0 10.9 %collective-permute-start.4 = (bf16[256,579]{1,0:T(8,128)(2,1)S(1)}, bf16[256,579]{1,0:T(8,128)(2,1)S(1)}, u32[]{:S(2)}, u32[]{:S(2)}) collective-permute-start(bf16[256,579]{1,0:T(8,128)(2,1)S(1)} %collective-permute-done.3.refs_2_), channel_id=1, source_target_pairs={{0,14},{2,0},{4,2},{6,4},{8,6},{10,8},{12,10},{14,12},{1,15},{3,1}... | collective-permute-start | bytes 889352 | tf_op jit(solution)/shard_map/ppermute | solution.py:26
  61.7 11.5 %collective-permute-start.2 = (bf16[256,579]{1,0:T(8,128)(2,1)S(1)}, bf16[256,579]{1,0:T(8,128)(2,1)S(1)}, u32[]{:S(2)}, u32[]{:S(2)}) collective-permute-start(bf16[256,579]{1,0:T(8,128)(2,1)S(1)} %collective-permute-done.1.refs_3_), channel_id=1, source_target_pairs={{0,2},{2,4},{4,6},{6,8},{8,10},{10,12},{12,14},{14,0},{1,3},{3,5},... | collective-permute-start | bytes 889352 | tf_op jit(solution)/shard_map/ppermute | solution.py:26
  67.9 13.3 %collective-permute-start.5 = (bf16[256,579]{1,0:T(8,128)(2,1)S(1)}, bf16[256,579]{1,0:T(8,128)(2,1)S(1)}, u32[]{:S(2)}, u32[]{:S(2)}) collective-permute-start(bf16[256,579]{1,0:T(8,128)(2,1)S(1)} %collective-permute-done.4.refs_4_), channel_id=1, source_target_pairs={{0,14},{2,0},{4,2},{6,4},{8,6},{10,8},{12,10},{14,12},{1,15},{3,1}... | collective-permute-start | bytes 889352 | tf_op jit(solution)/shard_map/ppermute | solution.py:26
  73.2 10.4 %collective-permute-start.6 = (bf16[256,579]{1,0:T(8,128)(2,1)S(1)}, bf16[256,579]{1,0:T(8,128)(2,1)S(1)}, u32[]{:S(2)}, u32[]{:S(2)}) collective-permute-start(bf16[256,579]{1,0:T(8,128)(2,1)S(1)} %collective-permute-done.2.refs_0_), channel_id=1, source_target_pairs={{0,2},{2,4},{4,6},{6,8},{8,10},{10,12},{12,14},{14,0},{1,3},{3,5},... | collective-permute-start | bytes 889352 | tf_op jit(solution)/shard_map/ppermute | solution.py:26
  75.2 1.6 %copy-start.1 = (bf16[4096,256]{1,0:T(8,128)(2,1)S(1)}, bf16[4096,256]{1,0:T(8,128)(2,1)}, u32[]{:S(2)}) copy-start(bf16[4096,256]{1,0:T(8,128)(2,1)} %refs_4_.1) | copy-start | bytes 6291460
  87.3 6.7 %collective-permute-start.9 = (f32[256,640]{1,0:T(8,128)}, f32[256,640]{1,0:T(8,128)S(1)}, u32[]{:S(2)}, u32[]{:S(2)}) collective-permute-start(f32[256,640]{1,0:T(8,128)} %get-tuple-element.10), channel_id=1, source_target_pairs={{0,1},{1,0},{2,3},{3,2},{4,5},{5,4},{6,7},{7,6},{8,9},{9,8},{10,11... | collective-permute-start | bytes 1966088 | tf_op jit(solution)/shard_map/ppermute | solution.py:26
  110.1 16.7 %all-to-all-start.2 = ((f32[16,4,256]{2,1,0:T(4,128)}), f32[16,4,256]{2,1,0:T(4,128)S(1)}, u32[]{:S(2)}, u32[]{:S(2)}) async-start(f32[16,4,256]{2,1,0:T(4,128)} %broadcast_in_dim.87), calls=%async_computation.2 | async-start | bytes 131072 | tf_op jit(solution)/shard_map/all_to_all | solution.py:21
where the time goes:
time: 129 us
  starting transfers between devices  56.8 us (44%)
  waiting for transfers between devices  36.1 us (28%)
  blocking collectives  13.4 us (10%)
  Pallas kernels  9.94 us (8%)
  local copies, waits for them, and re-layouts  7.02 us (5%)
  other arithmetic  3.29 us (3%)
    ppermute x10, starting transfers between devices, shifted(): lax.ppermute(array, axis, [(i, (i + by) % count) for i in range(count)])  40.1 us
    all_to_all x1, waiting for transfers between devices, on_device(): everyone = lax.all_to_all(packed, DP, 0, 0)  14.2 us
    ppermute x10, waiting for transfers between devices, shifted(): lax.ppermute(array, axis, [(i, (i + by) % count) for i in range(count)])  14.2 us
    all_to_all x1, blocking collectives, spread(): lax.all_to_all(jnp.broadcast_to(array, (count, *array.shape)), axes, 0, 0)  13.4 us
    all_to_all x1, starting transfers between devices, spread(): lax.all_to_all(jnp.broadcast_to(array, (count, *array.shape)), axes, 0, 0)  8.96 us
    pallas_call x2, Pallas kernels, block_products(): pl.pallas_call(functools.partial(block_kernel, offsets, had, t_width, s_w...  8.18 us
    all_to_all x1, starting transfers between devices, on_device(): everyone = lax.all_to_all(packed, DP, 0, 0)  7.8 us
    all_to_all x1, waiting for transfers between devices, spread(): lax.all_to_all(jnp.broadcast_to(array, (count, *array.shape)), axes, 0, 0)  7.77 us
  transfers between devices with their start and end apart: 12, of which 6 were waited for; matrix products, arithmetic and copies ran while one was open for 2% of the time, Pallas kernels for 5%

commit v1 on v0

--- a/solution.py
+++ b/solution.py
@@ -31,7 +31,8 @@
     found = [(0, piece)]
     ahead = behind = piece
     for k in range(1, count // 2):
-        ahead, behind = shifted(ahead, axis, 1), shifted(behind, axis, -1)
+        ahead = shifted(ahead, axis, 1)
+        behind = shifted(behind, axis, -1)
         found += [(-k, ahead), (k, behind)]
     return found + [(-(count // 2), shifted(ahead, axis, 1))]
 
@@ -152,7 +153,7 @@
             pltpu.VMEM((n, s_width, vocab), bf16),
             pltpu.SemaphoreType.DMA((n, 4)),
         ],
-        compiler_params=pltpu.CompilerParams(vmem_limit_bytes=24 << 20),
+        compiler_params=pltpu.CompilerParams(vmem_limit_bytes=48 << 20),
         cost_estimate=pl.CostEstimate(
             flops=4 * n * rows * vocab * (t_width + s_width),
             bytes_accessed=4 * n * vocab * (t_width + s_width),
@@ -207,7 +208,7 @@
         out_shape=jax.ShapeDtypeStruct((dp_count, half, 2 * s_width + t_width), jnp.bfloat16),
         in_specs=[SMEM, VMEM, VMEM],
         out_specs=VMEM,
-        compiler_params=pltpu.CompilerParams(vmem_limit_bytes=8 << 20),
+        compiler_params=pltpu.CompilerParams(vmem_limit_bytes=62 << 20),
     )(lengths, teacher_hidden, student_hidden)
     t_blocks = teacher_head.reshape(y_count, core_count, t_width, vocab_local)
     s_blocks = student_head.reshape(y_count, core_count, s_width, vocab_local)
@@ -229,9 +230,9 @@
     )(jnp.broadcast_to(row_source[:, None], (rows, 128)), gains, everyone.reshape(rows, -1))
 
     found = ring_pieces(piece, "tensor_0")
-    early = 1 + 2 * 2
-    mine, sent = block_products(found[:early], heads, None)
-    mine, sent = block_products(found[early:], heads, (mine, sent))
+    parts = block_products(found[:3], heads, None)
+    parts = block_products(found[3:-1], heads, parts)
+    mine, sent = block_products(found[-1:], heads, parts)
     squares = sent[:, 2 * vocab_local :][:, :1]
     got = shifted(sent, "tensor_1", 1)
     mean_square = (squares + got[:, 2 * vocab_local :][:, :1]) / (t_width * tensor_count)

time: 129 us -> 126 us (0.977)
  local copies, waits for them, and re-layouts: 7.02 us -> 5.39 us
  Pallas kernels: 9.94 us -> 8.62 us
    unnamed x16 -> x8, local copies, waits for them, and re-layouts: 1.62 us -> 0.02 us
    pallas_call x2 -> x3, Pallas kernels: 8.18 us -> 6.66 us  [block_products(): pl.pallas_call(functools.partial(block_kernel, offsets, had, t_width, s_w...]
  transfers between devices with their start and end apart: 12 -> 12, of which waited for: 6 -> 7; matrix products, arithmetic and copies ran while one was open for 2% -> 2% of each run, Pallas kernels for 5% -> 6%
where the time goes in v1:
time: 126 us; the launch traced here: 125 us
  starting transfers between devices  56.6 us (45%)
  waiting for transfers between devices  36.7 us (29%)
  blocking collectives  13.4 us (11%)
  Pallas kernels  8.62 us (7%)
  local copies, waits for them, and re-layouts  5.39 us (4%)
  other arithmetic  2.39 us (2%)
    ppermute x10, starting transfers between devices, shifted(): lax.ppermute(array, axis, [(i, (i + by) % count) for i in range(count)])  40.1 us
    ppermute x10, waiting for transfers between devices, shifted(): lax.ppermute(array, axis, [(i, (i + by) % count) for i in range(count)])  14.7 us
    all_to_all x1, waiting for transfers between devices, on_device(): everyone = lax.all_to_all(packed, DP, 0, 0)  14.2 us
    all_to_all x1, blocking collectives, spread(): lax.all_to_all(jnp.broadcast_to(array, (count, *array.shape)), axes, 0, 0)  13.4 us
    all_to_all x1, starting transfers between devices, spread(): lax.all_to_all(jnp.broadcast_to(array, (count, *array.shape)), axes, 0, 0)  8.95 us
    all_to_all x1, waiting for transfers between devices, spread(): lax.all_to_all(jnp.broadcast_to(array, (count, *array.shape)), axes, 0, 0)  7.77 us
    all_to_all x1, starting transfers between devices, on_device(): everyone = lax.all_to_all(packed, DP, 0, 0)  7.54 us
    pallas_call x3, Pallas kernels, block_products(): pl.pallas_call(functools.partial(block_kernel, offsets, had, t_width, s_w...  6.66 us
  transfers between devices with their start and end apart: 12, of which 7 were waited for; matrix products, arithmetic and copies ran while one was open for 2% of the time, Pallas kernels for 6%

profile of v1, /device:TPU:1, one launch (start us, length us, event | category | flops | bytes accessed | tf_op | source)
XLA Modules:
  0.0 125.1 jit_solution(11450589628261493313)
XLA Ops:
  0.7 2.5 %dynamic-slice_bitcast_fusion = bf16[8,320,256]{2,1,0:T(8,128)(2,1)} fusion(bf16[8,2,320,256]{3,2,1,0:T(8,128)(2,1)} %bitcast.60, s32[]{:T(128)S(6)} %select_n.51), kind=kLoop, calls=%fused_computation | loop fusion | bytes 2621444 | tf_op jit(solution)/shard_map/jit(dynamic_index_in_dim)/squeeze | solution.py:215
  3.2 8.7 %collective-permute-start.4 = (bf16[8,320,256]{2,1,0:T(8,128)(2,1)}, bf16[8,320,256]{2,1,0:T(8,128)(2,1)S(1)}, u32[]{:S(2)}, u32[]{:S(2)}) collective-permute-start(bf16[8,320,256]{2,1,0:T(8,128)(2,1)} %dynamic-slice_bitcast_fusion), channel_id=1, source_target_pairs={{0,1},{1,0},{2,3},{3,2},{4,5},{5,4},{6,7},{7,6},{8,9},{9,8},{10,11... | collective-permute-start | bytes 3932168 | tf_op jit(solution)/shard_map/ppermute | solution.py:26
  11.9 1.7 %shard_map.103 = bf16[32,8,832]{2,1,0:T(8,128)(2,1)} custom-call(s32[64]{0:T(128)} %lengths.1, bf16[16,320]{1,0:T(8,128)(2,1)} %teacher.1, bf16[16,256]{1,0:T(8,128)(2,1)} %student.1), custom_call_target="tpu_custom_call" | custom-call | tf_op jit(solution)/shard_map/pallas_call | solution.py:206
  13.6 7.5 %all-to-all-start = ((bf16[32,8,832]{2,1,0:T(8,128)(2,1)}), bf16[32,8,832]{2,1,0:T(8,128)(2,1)S(1)}, u32[]{:S(2)}, u32[]{:S(2)}) async-start(bf16[32,8,832]{2,1,0:T(8,128)(2,1)} %shard_map.103), calls=%async_computation | async-start | bytes 917504 | tf_op jit(solution)/shard_map/all_to_all | solution.py:219
  21.1 0.1 reshape.293
  21.2 0.2 slice_reduce_fusion.3
  21.4 0.1 lt.71
  21.5 0.1 lt.72
  21.6 0.1 lt.69
  21.7 0.1 lt.75
  21.8 0.1 lt.76
  21.9 0.1 add.158
  21.9 0.1 add.159
  22.0 0.1 sub.113
  22.1 0.1 reshape.294.gains
  22.3 0.3 select_reduce_fusion
  22.5 14.2 %all-to-all-done = bf16[32,8,832]{2,1,0:T(8,128)(2,1)S(1)} async-done(((bf16[32,8,832]{2,1,0:T(8,128)(2,1)}), bf16[32,8,832]{2,1,0:T(8,128)(2,1)S(1)}, u32[]{:S(2)}, u32[]{:S(2)}) %all-to-all-start) | async-done | bytes 426016 | tf_op jit(solution)/shard_map/all_to_all | solution.py:219
  36.7 0.1 broadcast_in_dim.83.source
  36.8 0.3 shard_map.104.refs_0_
  37.1 3.2 %collective-permute-start = (bf16[256,579]{1,0:T(8,128)(2,1)S(1)}, bf16[256,579]{1,0:T(8,128)(2,1)S(1)}, u32[]{:S(2)}, u32[]{:S(2)}) collective-permute-start(bf16[256,579]{1,0:T(8,128)(2,1)S(1)} %shard_map.104.refs_0_), channel_id=1, source_target_pairs={{0,2},{2,4},{4,6},{6,8},{8,10},{10,12},{12,14},{14,0},{1,3},{3,5},... | collective-permute-start | bytes 889352 | tf_op jit(solution)/shard_map/ppermute | solution.py:26
  40.3 1.3 %dynamic-slice_bitcast_fusion.1 = bf16[8,256,256]{2,1,0:T(8,128)(2,1)S(1)} fusion(bf16[8,2,256,256]{3,2,1,0:T(8,128)(2,1)} %bitcast.61, s32[]{:T(128)S(6)} %select_n.51), kind=kLoop, calls=%fused_computation.2 | loop fusion | bytes 2097156 | tf_op jit(solution)/shard_map/jit(dynamic_index_in_dim)/squeeze | solution.py:215
  41.6 4.0 %collective-permute-start.5 = (bf16[8,256,256]{2,1,0:T(8,128)(2,1)S(1)}, bf16[8,256,256]{2,1,0:T(8,128)(2,1)S(1)}, u32[]{:S(2)}, u32[]{:S(2)}) collective-permute-start(bf16[8,256,256]{2,1,0:T(8,128)(2,1)S(1)} %dynamic-slice_bitcast_fusion.1), channel_id=1, source_target_pairs={{0,1},{1,0},{2,3},{3,2},{4,5},{5,4},{6,7},{7,6},{8,9},{9,8},{10,11... | collective-permute-start | bytes 3145736 | tf_op jit(solution)/shard_map/ppermute | solution.py:26
  45.7 3.5 %collective-permute-start.6 = (bf16[256,579]{1,0:T(8,128)(2,1)S(1)}, bf16[256,579]{1,0:T(8,128)(2,1)S(1)}, u32[]{:S(2)}, u32[]{:S(2)}) collective-permute-start(bf16[256,579]{1,0:T(8,128)(2,1)S(1)} %shard_map.104.refs_0_), channel_id=1, source_target_pairs={{0,14},{2,0},{4,2},{6,4},{8,6},{10,8},{12,10},{14,12},{1,15},{3,1}... | collective-permute-start | bytes 889352 | tf_op jit(solution)/shard_map/ppermute | solution.py:26
  49.2 1.9 %collective-permute-start.1 = (bf16[256,579]{1,0:T(8,128)(2,1)S(1)}, bf16[256,579]{1,0:T(8,128)(2,1)S(1)}, u32[]{:S(2)}, u32[]{:S(2)}) collective-permute-start(bf16[256,579]{1,0:T(8,128)(2,1)S(1)} %collective-permute-done.refs_1_), channel_id=1, source_target_pairs={{0,2},{2,4},{4,6},{6,8},{8,10},{10,12},{12,14},{14,0},{1,3},{3,5},... | collective-permute-start | bytes 889352 | tf_op jit(solution)/shard_map/ppermute | solution.py:26
  51.1 5.7 %collective-permute-done.6.refs_2_ = bf16[256,579]{1,0:T(8,128)(2,1)S(1)} collective-permute-done((bf16[256,579]{1,0:T(8,128)(2,1)S(1)}, bf16[256,579]{1,0:T(8,128)(2,1)S(1)}, u32[]{:S(2)}, u32[]{:S(2)}) %collective-permute-start.6) | collective-permute-done | bytes 296480 | tf_op jit(solution)/shard_map/ppermute | solution.py:26
  56.8 4.7 %collective-permute-start.7 = (bf16[256,579]{1,0:T(8,128)(2,1)S(1)}, bf16[256,579]{1,0:T(8,128)(2,1)S(1)}, u32[]{:S(2)}, u32[]{:S(2)}) collective-permute-start(bf16[256,579]{1,0:T(8,128)(2,1)S(1)} %collective-permute-done.6.refs_2_), channel_id=1, source_target_pairs={{0,14},{2,0},{4,2},{6,4},{8,6},{10,8},{12,10},{14,12},{1,15},{3,1}... | collective-permute-start | bytes 889352 | tf_op jit(solution)/shard_map/ppermute | solution.py:26
  61.6 1.9 %collective-permute-start.2 = (bf16[256,579]{1,0:T(8,128)(2,1)S(1)}, bf16[256,579]{1,0:T(8,128)(2,1)S(1)}, u32[]{:S(2)}, u32[]{:S(2)}) collective-permute-start(bf16[256,579]{1,0:T(8,128)(2,1)S(1)} %collective-permute-done.1.refs_0_), channel_id=1, source_target_pairs={{0,2},{2,4},{4,6},{6,8},{8,10},{10,12},{12,14},{14,0},{1,3},{3,5},... | collective-permute-start | bytes 889352 | tf_op jit(solution)/shard_map/ppermute | solution.py:26
  63.5 4.2 %collective-permute-done.7.refs_1_ = bf16[256,579]{1,0:T(8,128)(2,1)S(1)} collective-permute-done((bf16[256,579]{1,0:T(8,128)(2,1)S(1)}, bf16[256,579]{1,0:T(8,128)(2,1)S(1)}, u32[]{:S(2)}, u32[]{:S(2)}) %collective-permute-start.7) | collective-permute-done | bytes 296480 | tf_op jit(solution)/shard_map/ppermute | solution.py:26
  67.7 5.3 %collective-permute-start.8 = (bf16[256,579]{1,0:T(8,128)(2,1)S(1)}, bf16[256,579]{1,0:T(8,128)(2,1)S(1)}, u32[]{:S(2)}, u32[]{:S(2)}) collective-permute-start(bf16[256,579]{1,0:T(8,128)(2,1)S(1)} %collective-permute-done.7.refs_1_), channel_id=1, source_target_pairs={{0,14},{2,0},{4,2},{6,4},{8,6},{10,8},{12,10},{14,12},{1,15},{3,1}... | collective-permute-start | bytes 889352 | tf_op jit(solution)/shard_map/ppermute | solution.py:26
  73.1 1.9 %collective-permute-start.3 = (bf16[256,579]{1,0:T(8,128)(2,1)S(1)}, bf16[256,579]{1,0:T(8,128)(2,1)S(1)}, u32[]{:S(2)}, u32[]{:S(2)}) collective-permute-start(bf16[256,579]{1,0:T(8,128)(2,1)S(1)} %collective-permute-done.2.refs_2_), channel_id=1, source_target_pairs={{0,2},{2,4},{4,6},{6,8},{8,10},{10,12},{12,14},{14,0},{1,3},{3,5},... | collective-permute-start | bytes 889352 | tf_op jit(solution)/shard_map/ppermute | solution.py:26
  75.0 2.4 %shard_map.105 = (f32[256,512]{1,0:T(8,128)S(1)}, f32[256,640]{1,0:T(8,128)S(1)}) custom-call(bf16[256,579]{1,0:T(8,128)(2,1)S(1)} %shard_map.104.refs_0_, bf16[256,579]{1,0:T(8,128)(2,1)S(1)} %collective-permute-done.refs_1_, bf16[256,579]{1,0:T(8,128)(2,1)S(1)} %collective-permute-done.6.refs_2_, bf16[5120,256]{1,0:T(8,128)(2,1)} %refs_1_.1, ...), custom_call_target="tpu_custom_call" | custom-call | flops 452984832 | bytes 1769472 | tf_op jit(solution)/shard_map/pallas_call | solution.py:141
  77.4 1.6 %collective-permute-done.8.refs_3_ = bf16[256,579]{1,0:T(8,128)(2,1)S(1)} collective-permute-done((bf16[256,579]{1,0:T(8,128)(2,1)S(1)}, bf16[256,579]{1,0:T(8,128)(2,1)S(1)}, u32[]{:S(2)}, u32[]{:S(2)}) %collective-permute-start.8) | collective-permute-done | bytes 296480 | tf_op jit(solution)/shard_map/ppermute | solution.py:26
  78.9 2.9 %shard_map.106 = (f32[256,512]{1,0:T(8,128)S(1)}, f32[256,640]{1,0:T(8,128)S(1)}) custom-call(bf16[256,579]{1,0:T(8,128)(2,1)S(1)} %collective-permute-done.1.refs_0_, bf16[256,579]{1,0:T(8,128)(2,1)S(1)} %collective-permute-done.7.refs_1_, bf16[256,579]{1,0:T(8,128)(2,1)S(1)} %collective-permute-done.2.refs_2_, ...), custom_call_target="tpu_custom_call" | custom-call | flops 603979776 | bytes 2359296 | tf_op jit(solution)/shard_map/pallas_call | solution.py:141
  81.8 1.6 %collective-permute-done.3.refs_0_ = bf16[256,579]{1,0:T(8,128)(2,1)S(1)} collective-permute-done((bf16[256,579]{1,0:T(8,128)(2,1)S(1)}, bf16[256,579]{1,0:T(8,128)(2,1)S(1)}, u32[]{:S(2)}, u32[]{:S(2)}) %collective-permute-start.3) | collective-permute-done | bytes 296480 | tf_op jit(solution)/shard_map/ppermute | solution.py:26
  83.4 1.4 %shard_map.107 = (f32[256,512]{1,0:T(8,128)S(1)}, f32[256,640]{1,0:T(8,128)S(1)}) custom-call(bf16[256,579]{1,0:T(8,128)(2,1)S(1)} %collective-permute-done.3.refs_0_, bf16[5120,256]{1,0:T(8,128)(2,1)} %refs_1_.1, bf16[4096,256]{1,0:T(8,128)(2,1)} %refs_2_.1, bf16[8,320,256]{2,1,0:T(8,128)(2,1)S(1)} %collective-permute-done.4.refs_5_.refs_6_.refs_3_, ...), custom_call_target="tpu_custom_call" | custom-call | flops 150994944 | bytes 589824 | tf_op jit(solution)/shard_map/pallas_call | solution.py:141
  84.8 4.8 %collective-permute-start.9 = (f32[256,640]{1,0:T(8,128)S(1)}, f32[256,640]{1,0:T(8,128)S(1)}, u32[]{:S(2)}, u32[]{:S(2)}) collective-permute-start(f32[256,640]{1,0:T(8,128)S(1)} %get-tuple-element.14), channel_id=1, source_target_pairs={{0,1},{1,0},{2,3},{3,2},{4,5},{5,4},{6,7},{7,6},{8,9},{9,8},{10,11... | collective-permute-start | bytes 1966088 | tf_op jit(solution)/shard_map/ppermute | solution.py:26
  89.6 1.7 %collective-permute-done.9 = f32[256,640]{1,0:T(8,128)S(1)} collective-permute-done((f32[256,640]{1,0:T(8,128)S(1)}, f32[256,640]{1,0:T(8,128)S(1)}, u32[]{:S(2)}, u32[]{:S(2)}) %collective-permute-start.9) | collective-permute-done | bytes 655392 | tf_op jit(solution)/shard_map/ppermute | solution.py:26
  91.3 0.1 fusion.7
  91.5 0.2 fusion.3
  91.7 0.4 fusion.1
  92.2 13.4 %all_to_all.15 = f32[32,4,256]{2,1,0:T(4,128)S(1)} all-to-all(f32[32,4,256]{2,1,0:T(4,128)S(1)} %broadcast_in_dim.86), channel_id=1, replica_groups=mesh['dp_0'=8,'dp_1'=4,'tensor_0'=8,'tensor_1'=2] {'dp_0','dp_1'}, dimensions={0} | all-to-all | bytes 262144 | tf_op jit(solution)/shard_map/all_to_all | solution.py:21
  105.6 0.1 slice_reduce_fusion.7
  105.8 0.6 broadcast_in_dim.87
  106.5 9.0 %all-to-all-start.2 = ((f32[16,4,256]{2,1,0:T(4,128)}), f32[16,4,256]{2,1,0:T(4,128)S(1)}, u32[]{:S(2)}, u32[]{:S(2)}) async-start(f32[16,4,256]{2,1,0:T(4,128)} %broadcast_in_dim.87), calls=%async_computation.2 | async-start | bytes 131072 | tf_op jit(solution)/shard_map/all_to_all | solution.py:21
  115.4 7.8 %all-to-all-done.2 = f32[16,4,256]{2,1,0:T(4,128)S(1)} async-done(((f32[16,4,256]{2,1,0:T(4,128)}), f32[16,4,256]{2,1,0:T(4,128)S(1)}, u32[]{:S(2)}, u32[]{:S(2)}) %all-to-all-start.2) | async-done | bytes 65568 | tf_op jit(solution)/shard_map/all_to_all | solution.py:21
  123.2 0.1 slice_reduce_fusion.2
  123.3 0.7 fusion.18
  124.0 1.1 convolution_convert_fusion
  (34 shorter events, 0.3 us)
Async XLA Ops:
  0.6 20.5 %copy-start.1 = (s32[64]{0:T(128)S(1)}, s32[64]{0:T(128)}, u32[]{:S(2)}) copy-start(s32[64]{0:T(128)} %lengths.1) | copy-start | bytes 772
  0.6 21.5 %copy-start = (f32[5120]{0:T(1024)S(1)}, f32[5120]{0:T(1024)}, u32[]{:S(2)}) copy-start(f32[5120]{0:T(1024)} %param.12) | copy-start | bytes 61444
  0.7 21.6 %copy-start.2 = (s32[512]{0:T(512)S(1)}, s32[512]{0:T(512)}, u32[]{:S(2)}) copy-start(s32[512]{0:T(512)} %param.15) | copy-start | bytes 6148
  0.7 21.6 %copy-start.3 = (s32[512]{0:T(512)S(1)}, s32[512]{0:T(512)}, u32[]{:S(2)}) copy-start(s32[512]{0:T(512)} %param.14) | copy-start | bytes 6148
  3.2 71.8 %collective-permute-start.4 = (bf16[8,320,256]{2,1,0:T(8,128)(2,1)}, bf16[8,320,256]{2,1,0:T(8,128)(2,1)S(1)}, u32[]{:S(2)}, u32[]{:S(2)}) collective-permute-start(bf16[8,320,256]{2,1,0:T(8,128)(2,1)} %dynamic-slice_bitcast_fusion), channel_id=1, source_target_pairs={{0,1},{1,0},{2,3},{3,2},{4,5},{5,4},{6,7},{7,6},{8,9},{9,8},{10,11... | collective-permute-start | bytes 3932168 | tf_op jit(solution)/shard_map/ppermute | solution.py:26
  13.6 23.1 %all-to-all-start = ((bf16[32,8,832]{2,1,0:T(8,128)(2,1)}), bf16[32,8,832]{2,1,0:T(8,128)(2,1)S(1)}, u32[]{:S(2)}, u32[]{:S(2)}) async-start(bf16[32,8,832]{2,1,0:T(8,128)(2,1)} %shard_map.103), calls=%async_computation | async-start | bytes 917504 | tf_op jit(solution)/shard_map/all_to_all | solution.py:219
  37.1 12.1 %collective-permute-start = (bf16[256,579]{1,0:T(8,128)(2,1)S(1)}, bf16[256,579]{1,0:T(8,128)(2,1)S(1)}, u32[]{:S(2)}, u32[]{:S(2)}) collective-permute-start(bf16[256,579]{1,0:T(8,128)(2,1)S(1)} %shard_map.104.refs_0_), channel_id=1, source_target_pairs={{0,2},{2,4},{4,6},{6,8},{8,10},{10,12},{12,14},{14,0},{1,3},{3,5},... | collective-permute-start | bytes 889352 | tf_op jit(solution)/shard_map/ppermute | solution.py:26
  41.6 33.4 %collective-permute-start.5 = (bf16[8,256,256]{2,1,0:T(8,128)(2,1)S(1)}, bf16[8,256,256]{2,1,0:T(8,128)(2,1)S(1)}, u32[]{:S(2)}, u32[]{:S(2)}) collective-permute-start(bf16[8,256,256]{2,1,0:T(8,128)(2,1)S(1)} %dynamic-slice_bitcast_fusion.1), channel_id=1, source_target_pairs={{0,1},{1,0},{2,3},{3,2},{4,5},{5,4},{6,7},{7,6},{8,9},{9,8},{10,11... | collective-permute-start | bytes 3145736 | tf_op jit(solution)/shard_map/ppermute | solution.py:26
  45.7 11.1 %collective-permute-start.6 = (bf16[256,579]{1,0:T(8,128)(2,1)S(1)}, bf16[256,579]{1,0:T(8,128)(2,1)S(1)}, u32[]{:S(2)}, u32[]{:S(2)}) collective-permute-start(bf16[256,579]{1,0:T(8,128)(2,1)S(1)} %shard_map.104.refs_0_), channel_id=1, source_target_pairs={{0,14},{2,0},{4,2},{6,4},{8,6},{10,8},{12,10},{14,12},{1,15},{3,1}... | collective-permute-start | bytes 889352 | tf_op jit(solution)/shard_map/ppermute | solution.py:26
  49.2 12.3 %collective-permute-start.1 = (bf16[256,579]{1,0:T(8,128)(2,1)S(1)}, bf16[256,579]{1,0:T(8,128)(2,1)S(1)}, u32[]{:S(2)}, u32[]{:S(2)}) collective-permute-start(bf16[256,579]{1,0:T(8,128)(2,1)S(1)} %collective-permute-done.refs_1_), channel_id=1, source_target_pairs={{0,2},{2,4},{4,6},{6,8},{8,10},{10,12},{12,14},{14,0},{1,3},{3,5},... | collective-permute-start | bytes 889352 | tf_op jit(solution)/shard_map/ppermute | solution.py:26
  56.8 10.9 %collective-permute-start.7 = (bf16[256,579]{1,0:T(8,128)(2,1)S(1)}, bf16[256,579]{1,0:T(8,128)(2,1)S(1)}, u32[]{:S(2)}, u32[]{:S(2)}) collective-permute-start(bf16[256,579]{1,0:T(8,128)(2,1)S(1)} %collective-permute-done.6.refs_2_), channel_id=1, source_target_pairs={{0,14},{2,0},{4,2},{6,4},{8,6},{10,8},{12,10},{14,12},{1,15},{3,1}... | collective-permute-start | bytes 889352 | tf_op jit(solution)/shard_map/ppermute | solution.py:26
  61.6 11.5 %collective-permute-start.2 = (bf16[256,579]{1,0:T(8,128)(2,1)S(1)}, bf16[256,579]{1,0:T(8,128)(2,1)S(1)}, u32[]{:S(2)}, u32[]{:S(2)}) collective-permute-start(bf16[256,579]{1,0:T(8,128)(2,1)S(1)} %collective-permute-done.1.refs_0_), channel_id=1, source_target_pairs={{0,2},{2,4},{4,6},{6,8},{8,10},{10,12},{12,14},{14,0},{1,3},{3,5},... | collective-permute-start | bytes 889352 | tf_op jit(solution)/shard_map/ppermute | solution.py:26
  67.7 11.2 %collective-permute-start.8 = (bf16[256,579]{1,0:T(8,128)(2,1)S(1)}, bf16[256,579]{1,0:T(8,128)(2,1)S(1)}, u32[]{:S(2)}, u32[]{:S(2)}) collective-permute-start(bf16[256,579]{1,0:T(8,128)(2,1)S(1)} %collective-permute-done.7.refs_1_), channel_id=1, source_target_pairs={{0,14},{2,0},{4,2},{6,4},{8,6},{10,8},{12,10},{14,12},{1,15},{3,1}... | collective-permute-start | bytes 889352 | tf_op jit(solution)/shard_map/ppermute | solution.py:26
  73.1 10.4 %collective-permute-start.3 = (bf16[256,579]{1,0:T(8,128)(2,1)S(1)}, bf16[256,579]{1,0:T(8,128)(2,1)S(1)}, u32[]{:S(2)}, u32[]{:S(2)}) collective-permute-start(bf16[256,579]{1,0:T(8,128)(2,1)S(1)} %collective-permute-done.2.refs_2_), channel_id=1, source_target_pairs={{0,2},{2,4},{4,6},{6,8},{8,10},{10,12},{12,14},{14,0},{1,3},{3,5},... | collective-permute-start | bytes 889352 | tf_op jit(solution)/shard_map/ppermute | solution.py:26
  84.8 6.5 %collective-permute-start.9 = (f32[256,640]{1,0:T(8,128)S(1)}, f32[256,640]{1,0:T(8,128)S(1)}, u32[]{:S(2)}, u32[]{:S(2)}) collective-permute-start(f32[256,640]{1,0:T(8,128)S(1)} %get-tuple-element.14), channel_id=1, source_target_pairs={{0,1},{1,0},{2,3},{3,2},{4,5},{5,4},{6,7},{7,6},{8,9},{9,8},{10,11... | collective-permute-start | bytes 1966088 | tf_op jit(solution)/shard_map/ppermute | solution.py:26
  106.5 16.7 %all-to-all-start.2 = ((f32[16,4,256]{2,1,0:T(4,128)}), f32[16,4,256]{2,1,0:T(4,128)S(1)}, u32[]{:S(2)}, u32[]{:S(2)}) async-start(f32[16,4,256]{2,1,0:T(4,128)} %broadcast_in_dim.87), calls=%async_computation.2 | async-start | bytes 131072 | tf_op jit(solution)/shard_map/all_to_all | solution.py:21
